TPU v7x, 32 devices: a whole 2x2x4 slice. The times are simulated.
32 devices in a mesh: img: 4 (over y, x), tpl: 8 (over z, core).
Axes of the slice: x: 2, y: 2, z: 4, core: 2. Of those that a mesh axis runs over, the one named last changes fastest.
Arguments:
- images: bfloat16 [6144, 2048], P(('img', 'tpl')), may hold values from -320 to 320
- templates: bfloat16 [3072, 2048], P('tpl'), may hold values from -0.62 to 0.62
- class_exponent: int32 [8], replicated, may hold values from 0 to 5
- class_mask: int32 [6144, 8], P('img'), may hold values from 0 to 1, as said below
Outputs:
- new_templates: float32 [3072, 2048], P('tpl', 'img')
- log_evidence: float32 [6144], P('img')
Inputs may be any that keep to these rules, and one draw needn't show every extreme that they name: `class_mask`: every image is compared with at least one class.
All inputs are finite; a program needn't handle non-finite values.
Results may differ from a plain program's by a relative error of at most 0.0023.
Values may be sent and summed in bfloat16 or wider, within the bound.
A program may use at most 64 MiB of HBM per device.

v0:
```python
import jax
import jax.numpy as jnp
from jax import lax
from jax.sharding import PartitionSpec as P

floor_score = -1e30


def per_device(images, templates, class_exponent, class_mask):
    tpl_rows = templates.shape[0]
    feature_count = templates.shape[1]
    class_count = class_exponent.shape[0]
    per_class = tpl_rows * lax.axis_size("tpl") // class_count
    global_rows = lax.axis_index("tpl") * tpl_rows + jnp.arange(tpl_rows, dtype=jnp.int32)
    owner = global_rows // per_class
    onehot = (jnp.arange(class_count, dtype=jnp.int32)[:, None] == owner[None, :]).astype(
        jnp.float32
    )
    inverse_temp = 0.5 * jnp.exp2(0.5 * class_exponent.astype(jnp.float32))
    template_beta = jnp.sum(onehot * inverse_temp[:, None], axis=0)
    allowed = jnp.dot(class_mask.astype(jnp.float32), onehot, precision=lax.Precision.HIGHEST) > 0.5
    squared_norm = jnp.sum(jnp.square(templates.astype(jnp.float32)), axis=1)
    gathered = lax.all_gather(images, "tpl", axis=0, tiled=True)
    raw = lax.dot_general(
        gathered, templates, (((1,), (1,)), ((), ())), preferred_element_type=jnp.float32
    )
    scores = template_beta[None, :] * (raw - 0.5 * squared_norm[None, :])
    local_top = jnp.max(jnp.where(allowed, scores, floor_score), axis=1)
    top = lax.pmax(local_top, "tpl")
    expo = jnp.where(allowed, jnp.exp(scores - top[:, None]), 0.0)
    totals = lax.psum(jnp.sum(expo, axis=1), "tpl")
    posterior = expo / totals[:, None]
    posterior_bf = posterior.astype(jnp.bfloat16)
    occupancy_part = jnp.sum(posterior, axis=0)
    weighted_part = lax.dot_general(
        posterior_bf, gathered, (((0,), (0,)), ((), ())), preferred_element_type=jnp.float32
    )
    columns = feature_count // lax.axis_size("img")
    col_start = lax.axis_index("img") * columns
    own_share = lax.psum_scatter(weighted_part, "img", scatter_dimension=1, tiled=True)
    occupancy = lax.psum(occupancy_part, "img")
    own_templates = lax.dynamic_slice_in_dim(templates, col_start, columns, 1).astype(jnp.float32)
    new_templates = (own_share + own_templates) / (occupancy[:, None] + 1.0)
    log_evidence = top + jnp.log(totals)
    return (new_templates, log_evidence)


def solution(mesh):
    in_specs = (P(("img", "tpl"), None), P("tpl", None), P(), P("img", None))
    out_specs = (P("tpl", "img"), P("img"))
    return jax.shard_map(
        per_device, mesh=mesh, in_specs=in_specs, out_specs=out_specs, check_vma=False
    )
```

profile of v0, /device:TPU:0, one launch (start us, length us, event | category | flops | bytes accessed | tf_op | source)
XLA Modules:
  0.0 171.4 jit_solution(5243481778394577077)
XLA Ops:
  7.2 0.0 all-gather.2.cloned.1.call-start
  7.2 0.7 all-gather.2.cloned.1.call-update
  7.9 0.0 reduce-scatter.2.cloned.1.call-start
  8.0 0.7 exponential_multiply_fusion
  8.6 0.1 select_reduce_fusion.1
  8.7 1.8 %multiply_reduce_fusion = f32[384]{0:T(512)S(1)} fusion(bf16[384,2048]{1,0:T(8,128)(2,1)} %param.5), kind=kLoop, calls=%fused_computation | loop fusion | flops 2358912 | bytes 1574400 | tf_op jit(solution)/shard_map/reduce_sum | solution.py:22
  10.5 0.0 copy-start
  10.5 66.5 %all-gather.2.cloned.1.call-done = bf16[1536,2048]{1,0:T(8,128)(2,1)} async-done(((bf16[192,2048]{1,0:T(8,128)(2,1)}), bf16[1536,2048]{1,0:T(8,128)(2,1)}) %all-gather.2.cloned.1.call-update) | async-done | bytes 6291472 | tf_op jit(solution)/shard_map/all_gather | solution.py:23
  77.1 5.2 %fusion = f32[1536,384]{0,1:T(8,128)S(1)} fusion(bf16[1536,2048]{1,0:T(8,128)(2,1)} %all-gather.2.cloned.1.call-done, bf16[384,2048]{1,0:T(8,128)(2,1)} %param.5, f32[384]{0:T(512)S(1)} %broadcast_multiply_fusion, f32[384]{0:T(512)S(1)} %select_reduce_fusion.1), kind=kOutput, calls=%fused_computation.2 | convolution fusion | flops 2417098752 | bytes 10226688 | tf_op jit(solution)/shard_map/dot_general | solution.py:24
  82.3 0.0 copy-done
  82.3 1.5 select_reduce_fusion
  83.8 14.4 %pmax.7 = f32[1536]{0:T(1024)S(1)} all-reduce(f32[1536]{0:T(1024)S(1)} %get-tuple-element.2), channel_id=1, replica_groups=mesh['img'=4,'tpl'=8] {'tpl'}, use_global_device_ids=true, to_apply=%region_3.4 | all-reduce | flops 1536 | bytes 12288 | tf_op jit(solution)/shard_map/pmax | solution.py:29
  98.3 0.6 fusion.3
  98.8 13.9 %psum.14 = f32[1536]{0:T(1024)S(1)} all-reduce(f32[1536]{0:T(1024)S(1)} %fusion.3), channel_id=1, replica_groups=mesh['img'=4,'tpl'=8] {'tpl'}, use_global_device_ids=true, to_apply=%region_5.6 | all-reduce | flops 1536 | bytes 12288 | tf_op jit(solution)/shard_map/psum | solution.py:31
  112.8 7.1 %fusion.4 = f32[384,2048]{1,0:T(8,128)} fusion(bf16[1536,2048]{1,0:T(8,128)(2,1)} %all-gather.2.cloned.1.call-done, pred[1536,384]{0,1:T(32,128)(4,1)S(1)} %get-tuple-element.3, f32[1536,384]{0,1:T(8,128)S(1)} %fusion, f32[1536]{0:T(1024)S(1)} %psum.14, f32[1536]{0:T(1024)S(1)} %pmax.7), kind=kOutput, calls=%fused_computation.9 | convolution fusion | flops 2418278400 | bytes 12398592 | tf_op jit(solution)/shard_map/dot_general | solution.py:35
  119.9 0.0 reduce-scatter.2.cloned.1.call-update
  119.9 0.7 fusion.6
  120.6 10.4 %psum.15 = f32[384]{0:T(512)S(1)} all-reduce(f32[384]{0:T(512)S(1)} %fusion.6), channel_id=1, replica_groups=mesh['img'=4,'tpl'=8] {'img'}, use_global_device_ids=true, to_apply=%region_8.9 | all-reduce | flops 384 | bytes 3072 | tf_op jit(solution)/shard_map/psum | solution.py:41
  131.0 0.6 log_add_fusion
  131.6 30.7 %reduce-scatter.2.cloned.1.call-done = f32[384,512]{1,0:T(8,128)} async-done(((f32[384,2048]{1,0:T(8,128)}), f32[384,512]{1,0:T(8,128)}) %reduce-scatter.2.cloned.1.call-update) | async-done | bytes 786448 | tf_op jit(solution)/shard_map/reduce_scatter | solution.py:40
  162.3 2.2 %add_divide_fusion = f32[384,512]{1,0:T(8,128)} fusion(f32[384,512]{1,0:T(8,128)} %reduce-scatter.2.cloned.1.call-done, f32[384]{0:T(512)S(1)} %broadcast_add_fusion, bf16[384,2048]{1,0:T(8,128)(2,1)} %param.5, s32[]{:T(128)S(6)} %select_n.22), kind=kLoop, calls=%fused_computation.11 | loop fusion | flops 589824 | bytes 1967620 | tf_op jit(solution)/shard_map/div | solution.py:43
  (3 shorter events, 0.0 us)
Async XLA Ops:
  7.2 69.9 %all-gather.2.cloned.1.call-start = ((), (), s32[]{:S(2)}) async-start(), calls=%async_computation.1 | async-start | bytes 7077888 | tf_op jit(solution)/shard_map/all_gather | solution.py:23
  7.9 154.4 %reduce-scatter.2.cloned.1.call-start = ((), (), s32[]{:S(2)}) async-start(), calls=%async_computation.2 | async-start | bytes 3932160 | tf_op jit(solution)/shard_map/reduce_scatter | solution.py:40
  10.5 71.8 %copy-start = (s32[1536,8]{0,1:T(8,128)S(1)}, s32[1536,8]{0,1:T(8,128)}, u32[]{:S(2)}) copy-start(s32[1536,8]{0,1:T(8,128)} %param.7) | copy-start | bytes 147460
Sparse Core Ops, SparseCore 0:
  9.6 67.4 all-gather.1
  120.0 42.2 reduce-scatter.1
where the time goes:
time: 172 us; the launch traced here: 171 us
  waiting for transfers between devices  97.9 us (57%)
  blocking collectives  38.7 us (23%)
  between operations  14.1 us (8%)
  matrix products  13.9 us (8%)
  other arithmetic  6.69 us (4%)
    all_gather x1, waiting for transfers between devices, per_device(): gathered = lax.all_gather(images, 'tpl', axis=0, tiled=True)  66.5 us
    reduce_scatter x1, waiting for transfers between devices, per_device(): lax.psum_scatter(weighted_part, 'img', scatter_dimension=1, tiled=True)  30.7 us
    pmax x1, blocking collectives, per_device(): top = lax.pmax(local_top, 'tpl')  14.4 us
    psum x1, blocking collectives, per_device(): totals = lax.psum(jnp.sum(expo, axis=1), 'tpl')  13.9 us
    psum x1, blocking collectives, per_device(): occupancy = lax.psum(occupancy_part, 'img')  10.4 us
    dot_general x1, matrix products, per_device(): lax.dot_general(posterior_bf, gathered, (((0,), (0,)), ((), ())), preferr...  7.11 us
    dot_general x1, matrix products, per_device(): lax.dot_general(gathered, templates, (((1,), (1,)), ((), ())), preferred_...  5.24 us
  transfers between devices with their start and end apart: 2, of which 2 were waited for; matrix products, arithmetic and copies ran while one was open for 2% of the time, Pallas kernels for 0%

commit v1 on v0

v1 whole, which is shorter than its diff:
```python
import functools

import jax
import jax.numpy as jnp
from jax import lax
from jax.experimental import pallas as pl
from jax.experimental.pallas import tpu as pltpu
from jax.sharding import PartitionSpec as P

MESH = pl.DeviceIdType.MESH
floor_score = -1e30


def kernel(
    n_img, n_tpl, x_ref, t_ref, beta_ref, mask_ref, out_ref, le_ref,
    imgs, e_ref, post_ref, st, acc, own, sbuf, rbuf, sqn, occ, obuf, orecv,
    img_send, img_recv, st_send, st_recv, rs_send, rs_recv, oc_send, oc_recv,
):
    chips = n_tpl // 2
    rows, feats = x_ref.shape
    cols = feats // n_img
    me_i, me_t = lax.axis_index("img"), lax.axis_index("tpl")
    chip, core = lax.div(me_t, 2), lax.rem(me_t, 2)
    sibling = 2 * chip + 1 - core

    def tpl_peer(off):
        return lax.rem(me_t + off, n_tpl)

    def img_peer(off):
        return lax.rem(me_i + off, n_img)

    barrier = pltpu.get_barrier_semaphore()
    for off in range(1, n_tpl):
        pl.semaphore_signal(barrier, inc=1, device_id={"tpl": tpl_peer(off)}, device_id_type=MESH)
    for off in range(1, n_img):
        pl.semaphore_signal(barrier, inc=1, device_id={"img": img_peer(off)}, device_id_type=MESH)
    pl.semaphore_wait(barrier, n_tpl - 1 + n_img - 1)

    def image_copy(src, block, way, to):
        return pltpu.make_async_remote_copy(
            src_ref=src, dst_ref=imgs.at[block], send_sem=img_send.at[way, lax.div(block, 2)],
            recv_sem=img_recv.at[block], device_id={"tpl": to}, device_id_type=MESH)

    right, left = me_t + 2, me_t - 2
    has_right, has_left = chip < chips - 1, chip > 0

    def forward(src, q):
        block = 2 * q + core

        @pl.when(jnp.logical_and(has_right, q <= chip))
        def _():
            image_copy(src, block, 0, right).start()

        @pl.when(jnp.logical_and(has_left, q >= chip))
        def _():
            image_copy(src, block, 1, left).start()

        image_copy(src, block, 2, sibling).start()

    forward(x_ref, chip)
    imgs[me_t] = x_ref[...]
    tf = t_ref[...].astype(jnp.float32)
    sqn[...] = 0.5 * jnp.sum(tf * tf, axis=1, keepdims=True)
    acc[...] = jnp.zeros_like(acc)
    occ[...] = jnp.zeros_like(occ)

    def stat_copy(q, off):
        return pltpu.make_async_remote_copy(
            src_ref=st.at[q, me_t], dst_ref=st.at[q, me_t], send_sem=st_send.at[q, off],
            recv_sem=st_recv.at[q, off], device_id={"tpl": tpl_peer(off)}, device_id_type=MESH)

    def stat_arrival(q, off):
        src = lax.rem(me_t + n_tpl - off, n_tpl)
        return pltpu.make_async_remote_copy(
            src_ref=st.at[q, src], dst_ref=st.at[q, src], send_sem=st_send.at[q, off],
            recv_sem=st_recv.at[q, off], device_id={"tpl": tpl_peer(off)}, device_id_type=MESH)

    def pair_of(q):
        return imgs[pl.ds(2 * q, 2)].reshape(2 * rows, feats)

    def score(q):
        raw = lax.dot_general(
            t_ref[...], pair_of(q), (((1,), (1,)), ((), ())), preferred_element_type=jnp.float32)
        s = beta_ref[...] * (raw - sqn[...])
        allowed = mask_ref[q] > 0.5
        top = jnp.max(jnp.where(allowed, s, floor_score), axis=0, keepdims=True)
        e = jnp.where(allowed, jnp.exp(s - top), 0.0)
        st[q, me_t, 0:1, :] = top
        st[q, me_t, 1:2, :] = jnp.sum(e, axis=0, keepdims=True)
        e_ref[q] = e
        for off in range(1, n_tpl):
            stat_copy(q, off).start()

    def wait_image(block):
        image_copy(imgs.at[block], block, 2, sibling).wait_recv()

    wait_image(2 * chip + 1 - core)
    score(chip)
    both = jnp.minimum(chip, chips - 1 - chip)

    def arrive(s, carry):
        near = lax.div(s + 1, 2)
        q_near = jnp.where(lax.rem(s, 2) == 1, chip - near, chip + near)
        far = s - both
        q_far = jnp.where(chip > chips - 1 - chip, chip - far, chip + far)
        q = jnp.where(s <= 2 * both, q_near, q_far)
        wait_image(2 * q + core)
        forward(imgs.at[2 * q + core], q)
        wait_image(2 * q + 1 - core)
        score(q)
        return carry

    lax.fori_loop(1, chips, arrive, 0)

    def consume(q):
        for off in range(1, n_tpl):
            stat_arrival(q, off).wait_recv()
        tops = [st[q, j, 0:1, :] for j in range(n_tpl)]
        top = functools.reduce(jnp.maximum, tops)
        total = sum(st[q, j, 1:2, :] * jnp.exp(tops[j] - top) for j in range(n_tpl))
        factor = jnp.exp(st[q, me_t, 0:1, :] - top) / total
        post = e_ref[q] * factor
        occ[...] += jnp.sum(post, axis=1, keepdims=True)
        post_ref[q] = post.astype(jnp.bfloat16)
        le_ref[q] = top + jnp.log(total)

    def middle(q, carry):
        consume(q)
        for j in range(n_img):
            part = slice(j * cols, (j + 1) * cols)
            block = imgs[pl.ds(2 * q, 2), :, part].reshape(2 * rows, cols)
            acc[:, part] += jnp.dot(post_ref[q], block, preferred_element_type=jnp.float32)
        return carry

    lax.fori_loop(1, chips - 1, middle, 0)
    ends = (0, chips - 1) if chips > 1 else (0,)
    for q in ends:
        consume(q)

    def occ_copy(off):
        return pltpu.make_async_remote_copy(
            src_ref=obuf, dst_ref=orecv.at[off], send_sem=oc_send.at[off],
            recv_sem=oc_recv.at[off], device_id={"img": img_peer(off)}, device_id_type=MESH)

    def sum_copy(off):
        return pltpu.make_async_remote_copy(
            src_ref=sbuf.at[off], dst_ref=rbuf.at[off], send_sem=rs_send.at[off],
            recv_sem=rs_recv.at[off], device_id={"img": img_peer(off)}, device_id_type=MESH)

    def share(off):
        part = pl.ds(pl.multiple_of(img_peer(off) * cols, cols), cols)
        value = acc[:, part]
        for q in ends:
            block = imgs[2 * q:2 * q + 2, :, part].reshape(2 * rows, cols)
            value += jnp.dot(post_ref[q], block, preferred_element_type=jnp.float32)
        return value

    tpl_rows = occ.shape[0]
    obuf[...] = jnp.transpose(jnp.broadcast_to(occ[...], (tpl_rows, 128)))[0:8]
    order = sorted(range(1, n_img), key=lambda off: abs(2 * off - n_img))
    for off in order:
        sbuf[off] = share(off).astype(jnp.bfloat16)
        sum_copy(off).start()
    for off in order:
        occ_copy(off).start()
    part = pl.ds(pl.multiple_of(me_i * cols, cols), cols)
    own[...] = share(0) + t_ref[:, part].astype(jnp.float32)
    occ_row = obuf[...]
    for off in range(1, n_img):
        occ_copy(off).wait_recv()
        occ_row += orecv[off]
    occ_col = jnp.transpose(jnp.broadcast_to(occ_row[0:1], (128, tpl_rows)))[:, 0:1]
    occ[...] = occ_col + 1.0
    total = own[...]
    for off in range(1, n_img):
        sum_copy(off).wait_recv()
        total += rbuf[off].astype(jnp.float32)
    out_ref[...] = total / occ[...]

    for off in range(1, n_img):
        occ_copy(off).wait_send()
        sum_copy(off).wait_send()

    def drain(q, carry):
        block = 2 * q + core

        @pl.when(jnp.logical_and(has_right, q <= chip))
        def _():
            image_copy(imgs.at[block], block, 0, right).wait_send()

        @pl.when(jnp.logical_and(has_left, q >= chip))
        def _():
            image_copy(imgs.at[block], block, 1, left).wait_send()

        image_copy(imgs.at[block], block, 2, sibling).wait_send()
        for off in range(1, n_tpl):
            stat_copy(q, off).wait_send()
        return carry

    lax.fori_loop(0, chips, drain, 0)


def solution(mesh):
    n_img, n_tpl = mesh.shape["img"], mesh.shape["tpl"]
    chips = n_tpl // 2

    def per_device(images, templates, class_exponent, class_mask):
        rows, feats = images.shape
        tpl_rows = templates.shape[0]
        cols = feats // n_img
        class_count = class_exponent.shape[0]
        per_class = tpl_rows * n_tpl // class_count
        first = lax.axis_index("tpl") * tpl_rows
        inverse_temp = 0.5 * jnp.exp2(0.5 * class_exponent.astype(jnp.float32))
        classes = jnp.arange(class_count, dtype=jnp.int32)
        owner = (first + jnp.arange(tpl_rows, dtype=jnp.int32)) // per_class
        onehot = (owner[:, None] == classes[None, :]).astype(jnp.float32)
        beta = jnp.sum(onehot * inverse_temp[None, :], axis=1, keepdims=True)
        if per_class % tpl_rows == 0:
            onehot = onehot[:1]
        mask = jnp.sum(jnp.where(onehot[:, :, None] > 0.5, class_mask.astype(jnp.float32).T[None], 0.0), axis=1)
        mask = mask.reshape(mask.shape[0], chips, 2 * rows).transpose(1, 0, 2)
        dma = pltpu.SemaphoreType.DMA
        vmem = pl.BlockSpec(memory_space=pltpu.VMEM)
        new, evidence = pl.pallas_call(
            functools.partial(kernel, n_img, n_tpl),
            out_shape=(
                jax.ShapeDtypeStruct((tpl_rows, cols), jnp.float32),
                jax.ShapeDtypeStruct((chips, 1, 2 * rows), jnp.float32),
            ),
            in_specs=[vmem] * 4,
            out_specs=(vmem, vmem),
            scratch_shapes=[
                pltpu.VMEM((n_tpl, rows, feats), jnp.bfloat16),
                pltpu.VMEM((chips, tpl_rows, 2 * rows), jnp.float32),
                pltpu.VMEM((chips, tpl_rows, 2 * rows), jnp.bfloat16),
                pltpu.VMEM((chips, n_tpl, 2, 2 * rows), jnp.float32),
                pltpu.VMEM((tpl_rows, feats), jnp.float32),
                pltpu.VMEM((tpl_rows, cols), jnp.float32),
                pltpu.VMEM((n_img, tpl_rows, cols), jnp.bfloat16),
                pltpu.VMEM((n_img, tpl_rows, cols), jnp.bfloat16),
                pltpu.VMEM((tpl_rows, 1), jnp.float32),
                pltpu.VMEM((tpl_rows, 1), jnp.float32),
                pltpu.VMEM((8, tpl_rows), jnp.float32),
                pltpu.VMEM((n_img, 8, tpl_rows), jnp.float32),
                dma((3, chips)),
                dma((n_tpl,)),
                dma((chips, n_tpl)),
                dma((chips, n_tpl)),
                dma((n_img,)),
                dma((n_img,)),
                dma((n_img,)),
                dma((n_img,)),
            ],
            compiler_params=pltpu.CompilerParams(
                collective_id=0, has_side_effects=True, vmem_limit_bytes=60 * 1024 * 1024),
        )(images, templates, beta, mask)
        return new, evidence.reshape(-1)

    in_specs = (P(("img", "tpl"), None), P("tpl", None), P(), P("img", None))
    out_specs = (P("tpl", "img"), P("img"))
    return jax.shard_map(
        per_device, mesh=mesh, in_specs=in_specs, out_specs=out_specs, check_vma=False
    )
```

time: 172 us -> 104 us (0.60)
  waiting for transfers between devices: 97.9 us -> 0 us
  Pallas kernels: 0 us -> 95.9 us
  blocking collectives: 38.7 us -> 0 us
  matrix products: 13.9 us -> 0 us
  between operations: 14.1 us -> 0.67 us
  local copies, waits for them, and re-layouts: 0.01 us -> 4.07 us
  other arithmetic: 6.69 us -> 2.64 us
    pallas_call x0 -> x1, Pallas kernels: none -> 95.9 us  [per_device(): pl.pallas_call(functools.partial(kernel, n_img, n_tpl), out_shape=(jax.Sh...]
    all_gather x1 -> x0, waiting for transfers between devices: 66.5 us -> none  [per_device(): gathered = lax.all_gather(images, 'tpl', axis=0, tiled=True)]
    reduce_scatter x1 -> x0, waiting for transfers between devices: 30.7 us -> none  [per_device(): lax.psum_scatter(weighted_part, 'img', scatter_dimension=1, tiled=True)]
    psum x2 -> x0, blocking collectives: 24.3 us -> none  [the longest x1 13.9 us: per_device(): totals = lax.psum(jnp.sum(expo, axis=1), 'tpl')]
    pmax x1 -> x0, blocking collectives: 14.4 us -> none  [per_device(): top = lax.pmax(local_top, 'tpl')]
    dot_general x3 -> x0, matrix products: 13.9 us -> none  [the longest x1 7.11 us: per_device(): lax.dot_general(posterior_bf, gathered, (((0,), (0,)), ((), ())), preferr...]
    div x1 -> x0, other arithmetic: 2.24 us -> none  [per_device(): new_templates = (own_share + own_templates) / (occupancy[:, None] + 1.0)]
    unnamed x2 -> x1, local copies, waits for them, and re-layouts: 0.01 us -> 2.06 us
  transfers between devices with their start and end apart: 2 -> 0, of which waited for: 2 -> 0; matrix products, arithmetic and copies ran while one was open for 2% -> 0% of each run, Pallas kernels for 0% -> 0%
where the time goes in v1:
time: 104 us; the launch traced here: 103 us
  Pallas kernels  95.9 us (92%)
  local copies, waits for them, and re-layouts  4.07 us (4%)
  other arithmetic  2.64 us (3%)
    pallas_call x1, Pallas kernels, per_device(): pl.pallas_call(functools.partial(kernel, n_img, n_tpl), out_shape=(jax.Sh...  95.9 us

profile of v1, /device:TPU:0, one launch (start us, length us, event | category | flops | bytes accessed | tf_op | source)
XLA Modules:
  0.0 103.3 jit_solution(14272825272796670250)
XLA Ops:
  0.6 0.7 exponential_multiply_fusion
  1.3 0.2 select_reduce_fusion
  1.5 0.1 iota_compare_fusion
  1.7 0.9 select_reduce_fusion.1
  2.6 0.6 transpose_reshape.3.mask_ref
  3.2 0.8 broadcast_in_dim.23.beta_ref
  4.0 95.9 %shard_map.59 = (f32[384,512]{1,0:T(8,128)}, f32[4,1,384]{2,1,0:T(1,128)}) custom-call(bf16[192,2048]{1,0:T(8,128)(2,1)} %x_ref.1, bf16[384,2048]{1,0:T(8,128)(2,1)} %t_ref.1, f32[384,1]{1,0:T(8,128)} %broadcast_in_dim.23.beta_ref, f32[4,1,384]{2,1,0:T(1,128)} %transpose_reshape.3.mask_ref), custom_call_target="tpu_custom_call" | custom-call | tf_op jit(solution)/shard_map/pallas_call | solution.py:225
  99.9 0.7 reduce.3
  100.6 0.6 reshape.34
  101.2 2.1 %copy.8 = f32[384,512]{1,0:T(8,128)} copy(f32[384,512]{1,0:T(8,128)} %get-tuple-element.8) | data formatting | bytes 1572864
  (2 shorter events, 0.0 us)

commit v2 on v1

--- a/solution.py
+++ b/solution.py
@@ -12,8 +12,8 @@
 
 
 def kernel(
-    n_img, n_tpl, x_ref, t_ref, beta_ref, mask_ref, out_ref, le_ref,
-    imgs, e_ref, post_ref, st, acc, own, sbuf, rbuf, sqn, occ, obuf, orecv,
+    n_img, n_tpl, parts, x_ref, t_ref, power_ref, mask_ref, out_ref, le_ref,
+    imgs, allow, le_row, e_ref, post_ref, st, acc, own, sbuf, rbuf, sqn, occ, obuf, orecv,
     img_send, img_recv, st_send, st_recv, rs_send, rs_recv, oc_send, oc_recv,
 ):
     chips = n_tpl // 2
@@ -36,28 +36,30 @@
         pl.semaphore_signal(barrier, inc=1, device_id={"img": img_peer(off)}, device_id_type=MESH)
     pl.semaphore_wait(barrier, n_tpl - 1 + n_img - 1)
 
-    def image_copy(src, block, way, to):
-        return pltpu.make_async_remote_copy(
-            src_ref=src, dst_ref=imgs.at[block], send_sem=img_send.at[way, lax.div(block, 2)],
-            recv_sem=img_recv.at[block], device_id={"tpl": to}, device_id_type=MESH)
+    size = rows // parts
+
+    def image_copy(src, block, k, way, to):
+        piece = pl.ds(k * size, size)
+        return pltpu.make_async_remote_copy(
+            src_ref=src.at[piece], dst_ref=imgs.at[block, piece],
+            send_sem=img_send.at[way, lax.div(block, 2), k],
+            recv_sem=img_recv.at[block, k], device_id={"tpl": to}, device_id_type=MESH)
 
     right, left = me_t + 2, me_t - 2
     has_right, has_left = chip < chips - 1, chip > 0
 
-    def forward(src, q):
-        block = 2 * q + core
-
-        @pl.when(jnp.logical_and(has_right, q <= chip))
-        def _():
-            image_copy(src, block, 0, right).start()
-
-        @pl.when(jnp.logical_and(has_left, q >= chip))
-        def _():
-            image_copy(src, block, 1, left).start()
-
-        image_copy(src, block, 2, sibling).start()
-
-    forward(x_ref, chip)
+    own_block = 2 * chip + core
+    for k in range(parts):
+        @pl.when(has_right)
+        def _():
+            image_copy(x_ref, own_block, k, 0, right).start()
+
+        @pl.when(has_left)
+        def _():
+            image_copy(x_ref, own_block, k, 1, left).start()
+
+        image_copy(x_ref, own_block, k, 2, sibling).start()
+
     imgs[me_t] = x_ref[...]
     tf = t_ref[...].astype(jnp.float32)
     sqn[...] = 0.5 * jnp.sum(tf * tf, axis=1, keepdims=True)
@@ -78,11 +80,36 @@
     def pair_of(q):
         return imgs[pl.ds(2 * q, 2)].reshape(2 * rows, feats)
 
+    class_count = power_ref.shape[0]
+    tpl_rows = t_ref.shape[0]
+    per_class = tpl_rows * n_tpl // class_count
+    pair = 2 * rows
+    first = me_t * tpl_rows
+    for q in range(chips):
+        allow[q] = mask_ref[:, q * pair:(q + 1) * pair]
+
+    def inverse_temp(c):
+        power = jnp.full((1, pair), power_ref[c], jnp.int32)
+        return 0.5 * jnp.exp2(0.5 * power.astype(jnp.float32))
+
+    if per_class % tpl_rows == 0:
+        only = lax.div(first, per_class)
+        beta = inverse_temp(only)
+
+        def allowed_at(q):
+            return allow[q, pl.ds(only, 1), :] > 0
+    else:
+        owner = lax.div(first + lax.broadcasted_iota(jnp.int32, (tpl_rows, pair), 0), per_class)
+        beta = sum(jnp.where(owner == c, inverse_temp(c), 0.0) for c in range(class_count))
+
+        def allowed_at(q):
+            return sum(jnp.where(owner == c, allow[q, c:c + 1, :], 0) for c in range(class_count)) > 0
+
     def score(q):
         raw = lax.dot_general(
             t_ref[...], pair_of(q), (((1,), (1,)), ((), ())), preferred_element_type=jnp.float32)
-        s = beta_ref[...] * (raw - sqn[...])
-        allowed = mask_ref[q] > 0.5
+        s = beta * (raw - sqn[...])
+        allowed = allowed_at(q)
         top = jnp.max(jnp.where(allowed, s, floor_score), axis=0, keepdims=True)
         e = jnp.where(allowed, jnp.exp(s - top), 0.0)
         st[q, me_t, 0:1, :] = top
@@ -91,23 +118,45 @@
         for off in range(1, n_tpl):
             stat_copy(q, off).start()
 
-    def wait_image(block):
-        image_copy(imgs.at[block], block, 2, sibling).wait_recv()
-
-    wait_image(2 * chip + 1 - core)
-    score(chip)
-    both = jnp.minimum(chip, chips - 1 - chip)
-
-    def arrive(s, carry):
-        near = lax.div(s + 1, 2)
-        q_near = jnp.where(lax.rem(s, 2) == 1, chip - near, chip + near)
-        far = s - both
-        q_far = jnp.where(chip > chips - 1 - chip, chip - far, chip + far)
-        q = jnp.where(s <= 2 * both, q_near, q_far)
-        wait_image(2 * q + core)
-        forward(imgs.at[2 * q + core], q)
-        wait_image(2 * q + 1 - core)
+    def wait_image(block, k):
+        image_copy(imgs.at[block], block, k, 2, sibling).wait_recv()
+
+    def relay(q, k, more, way, to):
+        block = 2 * q + core
+        wait_image(block, k)
+
+        @pl.when(more)
+        def _():
+            image_copy(imgs.at[block], block, k, way, to).start()
+
+        image_copy(imgs.at[block], block, k, 2, sibling).start()
+
+    def finish(q):
+        for k in range(parts):
+            wait_image(2 * q + 1 - core, k)
         score(q)
+
+    finish(chip)
+
+    def arrive(d, carry):
+        q_left, q_right = chip - d, chip + d
+        for k in range(parts):
+            @pl.when(q_left >= 0)
+            def _():
+                relay(q_left, k, has_right, 0, right)
+
+            @pl.when(q_right < chips)
+            def _():
+                relay(q_right, k, has_left, 1, left)
+
+        @pl.when(q_left >= 0)
+        def _():
+            finish(q_left)
+
+        @pl.when(q_right < chips)
+        def _():
+            finish(q_right)
+
         return carry
 
     lax.fori_loop(1, chips, arrive, 0)
@@ -122,7 +171,7 @@
         post = e_ref[q] * factor
         occ[...] += jnp.sum(post, axis=1, keepdims=True)
         post_ref[q] = post.astype(jnp.bfloat16)
-        le_ref[q] = top + jnp.log(total)
+        le_row[q] = top + jnp.log(total)
 
     def middle(q, carry):
         consume(q)
@@ -155,7 +204,8 @@
             value += jnp.dot(post_ref[q], block, preferred_element_type=jnp.float32)
         return value
 
-    tpl_rows = occ.shape[0]
+    for q in range(chips):
+        le_ref[:, q * pair:(q + 1) * pair] = le_row[q]
     obuf[...] = jnp.transpose(jnp.broadcast_to(occ[...], (tpl_rows, 128)))[0:8]
     order = sorted(range(1, n_img), key=lambda off: abs(2 * off - n_img))
     for off in order:
@@ -183,16 +233,16 @@
 
     def drain(q, carry):
         block = 2 * q + core
-
-        @pl.when(jnp.logical_and(has_right, q <= chip))
-        def _():
-            image_copy(imgs.at[block], block, 0, right).wait_send()
-
-        @pl.when(jnp.logical_and(has_left, q >= chip))
-        def _():
-            image_copy(imgs.at[block], block, 1, left).wait_send()
-
-        image_copy(imgs.at[block], block, 2, sibling).wait_send()
+        for k in range(parts):
+            @pl.when(jnp.logical_and(has_right, q <= chip))
+            def _():
+                image_copy(imgs.at[block], block, k, 0, right).wait_send()
+
+            @pl.when(jnp.logical_and(has_left, q >= chip))
+            def _():
+                image_copy(imgs.at[block], block, k, 1, left).wait_send()
+
+            image_copy(imgs.at[block], block, k, 2, sibling).wait_send()
         for off in range(1, n_tpl):
             stat_copy(q, off).wait_send()
         return carry
@@ -209,29 +259,21 @@
         tpl_rows = templates.shape[0]
         cols = feats // n_img
         class_count = class_exponent.shape[0]
-        per_class = tpl_rows * n_tpl // class_count
-        first = lax.axis_index("tpl") * tpl_rows
-        inverse_temp = 0.5 * jnp.exp2(0.5 * class_exponent.astype(jnp.float32))
-        classes = jnp.arange(class_count, dtype=jnp.int32)
-        owner = (first + jnp.arange(tpl_rows, dtype=jnp.int32)) // per_class
-        onehot = (owner[:, None] == classes[None, :]).astype(jnp.float32)
-        beta = jnp.sum(onehot * inverse_temp[None, :], axis=1, keepdims=True)
-        if per_class % tpl_rows == 0:
-            onehot = onehot[:1]
-        mask = jnp.sum(jnp.where(onehot[:, :, None] > 0.5, class_mask.astype(jnp.float32).T[None], 0.0), axis=1)
-        mask = mask.reshape(mask.shape[0], chips, 2 * rows).transpose(1, 0, 2)
+        parts = max(c for c in (4, 3, 2, 1) if rows % (16 * c) == 0 or c == 1)
         dma = pltpu.SemaphoreType.DMA
         vmem = pl.BlockSpec(memory_space=pltpu.VMEM)
         new, evidence = pl.pallas_call(
-            functools.partial(kernel, n_img, n_tpl),
+            functools.partial(kernel, n_img, n_tpl, parts),
             out_shape=(
                 jax.ShapeDtypeStruct((tpl_rows, cols), jnp.float32),
-                jax.ShapeDtypeStruct((chips, 1, 2 * rows), jnp.float32),
+                jax.ShapeDtypeStruct((1, n_tpl * rows), jnp.float32),
             ),
-            in_specs=[vmem] * 4,
+            in_specs=[vmem, vmem, pl.BlockSpec(memory_space=pltpu.SMEM), vmem],
             out_specs=(vmem, vmem),
             scratch_shapes=[
                 pltpu.VMEM((n_tpl, rows, feats), jnp.bfloat16),
+                pltpu.VMEM((chips, class_count, 2 * rows), jnp.int32),
+                pltpu.VMEM((chips, 1, 2 * rows), jnp.float32),
                 pltpu.VMEM((chips, tpl_rows, 2 * rows), jnp.float32),
                 pltpu.VMEM((chips, tpl_rows, 2 * rows), jnp.bfloat16),
                 pltpu.VMEM((chips, n_tpl, 2, 2 * rows), jnp.float32),
@@ -243,8 +285,8 @@
                 pltpu.VMEM((tpl_rows, 1), jnp.float32),
                 pltpu.VMEM((8, tpl_rows), jnp.float32),
                 pltpu.VMEM((n_img, 8, tpl_rows), jnp.float32),
-                dma((3, chips)),
-                dma((n_tpl,)),
+                dma((3, chips, parts)),
+                dma((n_tpl, parts)),
                 dma((chips, n_tpl)),
                 dma((chips, n_tpl)),
                 dma((n_img,)),
@@ -254,7 +296,7 @@
             ],
             compiler_params=pltpu.CompilerParams(
                 collective_id=0, has_side_effects=True, vmem_limit_bytes=60 * 1024 * 1024),
-        )(images, templates, beta, mask)
+        )(images, templates, class_exponent, class_mask.T)
         return new, evidence.reshape(-1)
 
     in_specs = (P(("img", "tpl"), None), P("tpl", None), P(), P("img", None))

time: 104 us -> 94.5 us (0.909)
  Pallas kernels: 95.9 us -> 90.2 us
  local copies, waits for them, and re-layouts: 4.07 us -> 2.06 us
  other arithmetic: 2.64 us -> 1.31 us
    pallas_call x1, Pallas kernels: 95.9 us -> 90.2 us  [per_device(): pl.pallas_call(functools.partial(kernel, n_img, n_tpl, parts), out_shape=...]
    reduce_sum x2 -> x0, other arithmetic: 1.12 us -> none  [the longest x1 0.89 us: per_device(): jnp.sum(jnp.where(onehot[:, :, None] > 0.5, class_mask.astype(jnp.float32...]
where the time goes in v2:
time: 94.5 us; the launch traced here: 94.2 us
  Pallas kernels  90.2 us (95%)
  local copies, waits for them, and re-layouts  2.06 us (2%)
  other arithmetic  1.31 us (1%)
    pallas_call x1, Pallas kernels, per_device(): pl.pallas_call(functools.partial(kernel, n_img, n_tpl, parts), out_shape=...  90.2 us
    unnamed x1, local copies, waits for them, and re-layouts  2.06 us

profile of v2, /device:TPU:0, one launch (start us, length us, event | category | flops | bytes accessed | tf_op | source)
XLA Modules:
  0.0 94.2 jit_solution(17858706147117899464)
XLA Ops:
  0.6 90.2 %shard_map.59 = (f32[384,512]{1,0:T(8,128)}, f32[1,1536]{1,0:T(1,128)}) custom-call(bf16[192,2048]{1,0:T(8,128)(2,1)} %x_ref.1, bf16[384,2048]{1,0:T(8,128)(2,1)} %t_ref.1, s32[8]{0:T(128)} %power_ref.1, s32[8,1536]{1,0:T(8,128)} %bitcast.1), custom_call_target="tpu_custom_call" | custom-call | tf_op jit(solution)/shard_map/pallas_call | solution.py:265
  90.9 1.3 %reduce = f32[1536]{0:T(1024)} reduce(f32[1,1536]{1,0:T(1,128)} %get-tuple-element.5, f32[]{:T(128)} %constant), dimensions={0}, to_apply=%get-tuple-element.5.reduce_sub_computation | reduce | bytes 12292 | tf_op jit(solution)/shard_map/pallas_call | solution.py:265
  92.2 2.1 %copy.7 = f32[384,512]{1,0:T(8,128)} copy(f32[384,512]{1,0:T(8,128)} %get-tuple-element.8) | data formatting | bytes 1572864

commit v3 on v2

--- a/solution.py
+++ b/solution.py
@@ -191,45 +191,71 @@
             src_ref=obuf, dst_ref=orecv.at[off], send_sem=oc_send.at[off],
             recv_sem=oc_recv.at[off], device_id={"img": img_peer(off)}, device_id_type=MESH)
 
-    def sum_copy(off):
-        return pltpu.make_async_remote_copy(
-            src_ref=sbuf.at[off], dst_ref=rbuf.at[off], send_sem=rs_send.at[off],
-            recv_sem=rs_recv.at[off], device_id={"img": img_peer(off)}, device_id_type=MESH)
-
-    def share(off):
-        part = pl.ds(pl.multiple_of(img_peer(off) * cols, cols), cols)
-        value = acc[:, part]
+    bits = [1 << k for k in range(n_img.bit_length() - 1)]
+    groups = len(bits) if bits and tpl_rows % (16 * len(bits)) == 0 else 1
+    depth = tpl_rows // groups
+    orders = [bits[g:] + bits[:g] for g in range(groups)]
+
+    def flip(mask):
+        return me_i + sum(b - 2 * b * lax.rem(lax.div(me_i, b), 2) for b in bits if b & mask)
+
+    def turn(g, mask):
+        return next(r for r, b in enumerate(orders[g]) if b & mask)
+
+    def band(g):
+        return slice(g * depth, (g + 1) * depth)
+
+    def sum_copy(g, mask):
+        return pltpu.make_async_remote_copy(
+            src_ref=sbuf.at[mask, band(g)], dst_ref=rbuf.at[mask, band(g)],
+            send_sem=rs_send.at[g, mask], recv_sem=rs_recv.at[g, mask],
+            device_id={"img": flip(orders[g][turn(g, mask)])}, device_id_type=MESH)
+
+    def share(g, mask):
+        part = pl.ds(pl.multiple_of(flip(mask) * cols, cols), cols)
+        value = acc[band(g), part]
         for q in ends:
             block = imgs[2 * q:2 * q + 2, :, part].reshape(2 * rows, cols)
-            value += jnp.dot(post_ref[q], block, preferred_element_type=jnp.float32)
+            value += jnp.dot(post_ref[q, band(g)], block, preferred_element_type=jnp.float32)
+        return value
+
+    def received(g, mask, rounds):
+        value = 0.0
+        for b in orders[g][:rounds]:
+            sum_copy(g, b + mask).wait_recv()
+            value += rbuf[b + mask, band(g)].astype(jnp.float32)
         return value
 
     for q in range(chips):
         le_ref[:, q * pair:(q + 1) * pair] = le_row[q]
     obuf[...] = jnp.transpose(jnp.broadcast_to(occ[...], (tpl_rows, 128)))[0:8]
-    order = sorted(range(1, n_img), key=lambda off: abs(2 * off - n_img))
-    for off in order:
-        sbuf[off] = share(off).astype(jnp.bfloat16)
-        sum_copy(off).start()
-    for off in order:
+    for off in range(1, n_img):
         occ_copy(off).start()
-    part = pl.ds(pl.multiple_of(me_i * cols, cols), cols)
-    own[...] = share(0) + t_ref[:, part].astype(jnp.float32)
-    occ_row = obuf[...]
-    for off in range(1, n_img):
-        occ_copy(off).wait_recv()
-        occ_row += orecv[off]
-    occ_col = jnp.transpose(jnp.broadcast_to(occ_row[0:1], (128, tpl_rows)))[:, 0:1]
-    occ[...] = occ_col + 1.0
-    total = own[...]
-    for off in range(1, n_img):
-        sum_copy(off).wait_recv()
-        total += rbuf[off].astype(jnp.float32)
-    out_ref[...] = total / occ[...]
+    masks = sorted(range(1, n_img), key=lambda mask: -mask.bit_count())
+    mine = pl.ds(pl.multiple_of(me_i * cols, cols), cols)
+    for r in range(len(bits)):
+        for mask in masks:
+            for g in range(groups):
+                if turn(g, mask) == r:
+                    value = share(g, mask)
+                    sbuf[mask, band(g)] = (value + received(g, mask, r)).astype(jnp.bfloat16)
+                    sum_copy(g, mask).start()
+        if r == 0:
+            for g in range(groups):
+                own[band(g)] = share(g, 0) + t_ref[band(g), mine].astype(jnp.float32)
+            occ_row = obuf[...]
+            for off in range(1, n_img):
+                occ_copy(off).wait_recv()
+                occ_row += orecv[off]
+            occ_col = jnp.transpose(jnp.broadcast_to(occ_row[0:1], (128, tpl_rows)))[:, 0:1]
+            occ[...] = occ_col + 1.0
+    for g in range(groups):
+        out_ref[band(g)] = (own[band(g)] + received(g, 0, len(bits))) / occ[band(g)]
 
     for off in range(1, n_img):
         occ_copy(off).wait_send()
-        sum_copy(off).wait_send()
+        for g in range(groups):
+            sum_copy(g, off).wait_send()
 
     def drain(q, carry):
         block = 2 * q + core
@@ -248,6 +274,11 @@
         return carry
 
     lax.fori_loop(0, chips, drain, 0)
+
+
+def emit(new_ref, evidence_ref, new_out, evidence_out):
+    new_out[...] = new_ref[...]
+    evidence_out[...] = evidence_ref[...].reshape(evidence_out.shape)
 
 
 def solution(mesh):
@@ -289,15 +320,23 @@
                 dma((n_tpl, parts)),
                 dma((chips, n_tpl)),
                 dma((chips, n_tpl)),
-                dma((n_img,)),
-                dma((n_img,)),
+                dma((n_img, n_img)),
+                dma((n_img, n_img)),
                 dma((n_img,)),
                 dma((n_img,)),
             ],
             compiler_params=pltpu.CompilerParams(
                 collective_id=0, has_side_effects=True, vmem_limit_bytes=60 * 1024 * 1024),
         )(images, templates, class_exponent, class_mask.T)
-        return new, evidence.reshape(-1)
+        return pl.pallas_call(
+            emit,
+            out_shape=(
+                jax.ShapeDtypeStruct(new.shape, jnp.float32),
+                jax.ShapeDtypeStruct((n_tpl * rows,), jnp.float32),
+            ),
+            in_specs=[vmem] * 2,
+            out_specs=(vmem, vmem),
+        )(new, evidence)
 
     in_specs = (P(("img", "tpl"), None), P("tpl", None), P(), P("img", None))
     out_specs = (P("tpl", "img"), P("img"))

time: 94.5 us -> 87.6 us (0.927)
  Pallas kernels: 90.2 us -> 86.8 us
  local copies, waits for them, and re-layouts: 2.06 us -> 0 us
  other arithmetic: 1.31 us -> 0 us
    pallas_call x1, Pallas kernels: 90.2 us -> 84.7 us  [per_device(): pl.pallas_call(functools.partial(kernel, n_img, n_tpl, parts), out_shape=...]
    pallas_call x0 -> x1, Pallas kernels: none -> 2.07 us  [per_device(): pl.pallas_call(emit, out_shape=(jax.ShapeDtypeStruct(new.shape, jnp.float...]
    unnamed x1 -> x0, local copies, waits for them, and re-layouts: 2.06 us -> none
    pallas_call x1 -> x0, other arithmetic: 1.31 us -> none  [per_device(): pl.pallas_call(functools.partial(kernel, n_img, n_tpl, parts), out_shape=...]
where the time goes in v3:
time: 87.6 us; the launch traced here: 87.4 us
  Pallas kernels  86.8 us (99%)
    pallas_call x1, Pallas kernels, per_device(): pl.pallas_call(functools.partial(kernel, n_img, n_tpl, parts), out_shape=...  84.7 us
    pallas_call x1, Pallas kernels, per_device(): pl.pallas_call(emit, out_shape=(jax.ShapeDtypeStruct(new.shape, jnp.float...  2.07 us

profile of v3, /device:TPU:0, one launch (start us, length us, event | category | flops | bytes accessed | tf_op | source)
XLA Modules:
  0.0 87.4 jit_solution(325887980510526383)
XLA Ops:
  0.6 84.7 %shard_map.59 = (f32[384,512]{1,0:T(8,128)}, f32[1,1536]{1,0:T(1,128)}) custom-call(bf16[192,2048]{1,0:T(8,128)(2,1)} %x_ref.1, bf16[384,2048]{1,0:T(8,128)(2,1)} %t_ref.1, s32[8]{0:T(128)} %power_ref.1, s32[8,1536]{1,0:T(8,128)} %bitcast.1), custom_call_target="tpu_custom_call" | custom-call | tf_op jit(solution)/shard_map/pallas_call | solution.py:296
  85.4 2.1 %shard_map.60 = (f32[384,512]{1,0:T(8,128)}, f32[1536]{0:T(1024)}) custom-call(f32[384,512]{1,0:T(8,128)} %get-tuple-element.4.new_ref, f32[1,1536]{1,0:T(1,128)} %get-tuple-element.5.evidence_ref), custom_call_target="tpu_custom_call" | custom-call | tf_op jit(solution)/shard_map/pallas_call | solution.py:331

commit v4 on v3

--- a/solution.py
+++ b/solution.py
@@ -12,8 +12,8 @@
 
 
 def kernel(
-    n_img, n_tpl, parts, x_ref, t_ref, power_ref, mask_ref, out_ref, le_ref,
-    imgs, allow, le_row, e_ref, post_ref, st, acc, own, sbuf, rbuf, sqn, occ, obuf, orecv,
+    n_img, n_tpl, parts, x_ref, t_hbm, power_ref, mask_hbm, out_ref, le_ref,
+    t_ref, mask_ref, loads, imgs, allow, le_row, e_ref, post_ref, st, acc, own, sbuf, rbuf, sqn, occ, obuf, orecv,
     img_send, img_recv, st_send, st_recv, rs_send, rs_recv, oc_send, oc_recv,
 ):
     chips = n_tpl // 2
@@ -34,6 +34,11 @@
         pl.semaphore_signal(barrier, inc=1, device_id={"tpl": tpl_peer(off)}, device_id_type=MESH)
     for off in range(1, n_img):
         pl.semaphore_signal(barrier, inc=1, device_id={"img": img_peer(off)}, device_id_type=MESH)
+    load_t = pltpu.make_async_copy(t_hbm, t_ref, loads.at[0])
+    load_x = pltpu.make_async_copy(x_ref, imgs.at[me_t], loads.at[1])
+    load_mask = pltpu.make_async_copy(mask_hbm, mask_ref, loads.at[2])
+    for load in (load_t, load_x, load_mask):
+        load.start()
     pl.semaphore_wait(barrier, n_tpl - 1 + n_img - 1)
 
     size = rows // parts
@@ -60,7 +65,8 @@
 
         image_copy(x_ref, own_block, k, 2, sibling).start()
 
-    imgs[me_t] = x_ref[...]
+    for load in (load_t, load_x, load_mask):
+        load.wait()
     tf = t_ref[...].astype(jnp.float32)
     sqn[...] = 0.5 * jnp.sum(tf * tf, axis=1, keepdims=True)
     acc[...] = jnp.zeros_like(acc)
@@ -293,15 +299,19 @@
         parts = max(c for c in (4, 3, 2, 1) if rows % (16 * c) == 0 or c == 1)
         dma = pltpu.SemaphoreType.DMA
         vmem = pl.BlockSpec(memory_space=pltpu.VMEM)
+        far = pl.BlockSpec(memory_space=pl.ANY)
         new, evidence = pl.pallas_call(
             functools.partial(kernel, n_img, n_tpl, parts),
             out_shape=(
                 jax.ShapeDtypeStruct((tpl_rows, cols), jnp.float32),
                 jax.ShapeDtypeStruct((1, n_tpl * rows), jnp.float32),
             ),
-            in_specs=[vmem, vmem, pl.BlockSpec(memory_space=pltpu.SMEM), vmem],
+            in_specs=[far, far, pl.BlockSpec(memory_space=pltpu.SMEM), far],
             out_specs=(vmem, vmem),
             scratch_shapes=[
+                pltpu.VMEM((tpl_rows, feats), jnp.bfloat16),
+                pltpu.VMEM((class_count, n_tpl * rows), jnp.int32),
+                dma((3,)),
                 pltpu.VMEM((n_tpl, rows, feats), jnp.bfloat16),
                 pltpu.VMEM((chips, class_count, 2 * rows), jnp.int32),
                 pltpu.VMEM((chips, 1, 2 * rows), jnp.float32),

time: 87.6 us -> 86.9 us (level)
  no operation moved by 1% of the time
where the time goes in v4:
time: 86.9 us; the launch traced here: 86.7 us
  Pallas kernels  86.1 us (99%)
    pallas_call x1, Pallas kernels, per_device(): pl.pallas_call(functools.partial(kernel, n_img, n_tpl, parts), out_shape=...  84 us
    pallas_call x1, Pallas kernels, per_device(): pl.pallas_call(emit, out_shape=(jax.ShapeDtypeStruct(new.shape, jnp.float...  2.07 us

profile of v4, /device:TPU:0, one launch (start us, length us, event | category | flops | bytes accessed | tf_op | source)
XLA Modules:
  0.0 86.7 jit_solution(11017230535929776980)
XLA Ops:
  0.6 84.0 %shard_map.59 = (f32[384,512]{1,0:T(8,128)}, f32[1,1536]{1,0:T(1,128)}) custom-call(bf16[192,2048]{1,0:T(8,128)(2,1)} %x_ref.1, bf16[384,2048]{1,0:T(8,128)(2,1)} %t_hbm.1, s32[8]{0:T(128)} %power_ref.1, s32[8,1536]{1,0:T(8,128)} %bitcast.1), custom_call_target="tpu_custom_call" | custom-call | tf_op jit(solution)/shard_map/pallas_call | solution.py:303
  84.7 2.1 %shard_map.60 = (f32[384,512]{1,0:T(8,128)}, f32[1536]{0:T(1024)}) custom-call(f32[384,512]{1,0:T(8,128)} %get-tuple-element.4.new_ref, f32[1,1536]{1,0:T(1,128)} %get-tuple-element.5.evidence_ref), custom_call_target="tpu_custom_call" | custom-call | tf_op jit(solution)/shard_map/pallas_call | solution.py:341
